TPU v7x, 32 devices: a whole 2x2x4 slice. The times are simulated.
32 devices in a mesh: groups: 2 (over y), genome: 4 (over z), ancestry: 2 (over x), trait: 2 (over core).
Axes of the slice: x: 2, y: 2, z: 4, core: 2. Of those that a mesh axis runs over, the one named last changes fastest.
Arguments:
- zscores: float32 [2, 64, 8192], P('ancestry', 'trait', ('groups', 'genome')), parts along dimension 2
- ld_diag: bfloat16 [2, 8192, 1024], P('ancestry', ('groups', 'genome')), parts along dimension 1, as said below
- ld_next: bfloat16 [2, 8192, 1024], P('ancestry', ('groups', 'genome')), parts along dimension 1
- prior_precision: float32 [2, 2], replicated, as said below
- chrom_cut: int32 [8], P('groups'), parts along dimension 0, may hold values from 0 to 2047
- band_width: int32 [8], P('groups'), parts along dimension 0, may hold values from 512 to 2047
Outputs:
- effect_sizes: float32 [2, 64, 8192], P('ancestry', 'trait', ('groups', 'genome')), parts along dimension 2
There are 2 independent parts, one for each index of `groups`. A program takes and returns all parts, laid end to end along the dimension named above; an argument that names none is the same for every part. Nothing has to cross between parts.
Inputs may be any that keep to these rules, and one draw needn't show every extreme that they name: `chrom_cut`: an entry below 1024 is the offset within its block of the first variant of a new chromosome; 1024 or more means the block holds no chromosome start. `band_width`: LD between two variants counts only when their distance is below the smaller width of their two blocks. `ld_diag`: each 1024 x 1024 diagonal block is symmetric with a positive diagonal. `prior_precision`: symmetric; each diagonal entry exceeds the sum of the magnitudes of the other entries of its row.
All inputs are finite; a program needn't handle non-finite values.
Results may differ from a plain program's by a relative error of at most 0.0025.
Values may be sent and summed in bfloat16 or wider, within the bound.
A program may use at most 64 MiB of HBM per device.

v0:
```python
import jax
import jax.numpy as jnp
from jax import lax
from jax.sharding import PartitionSpec as P

ITERS = 3


def passed_along(value, axis, steps):
    count = lax.axis_size(axis)
    leading, last = (max(0, -steps), min(count, count - steps))
    return lax.ppermute(value, axis, [(source, source + steps) for source in range(leading, last)])


def block_masks(block_len, cut_here, cut_after, width_here, width_after):
    row_ids = jnp.arange(block_len, dtype=jnp.int32)[:, None]
    col_ids = jnp.arange(block_len, dtype=jnp.int32)[None, :]
    opened = cut_here < block_len
    same_chrom = opened & (row_ids >= cut_here) == opened & (col_ids >= cut_here)
    inside = (jnp.abs(row_ids - col_ids) < width_here) & same_chrom
    before_cut = opened & (row_ids < cut_here)
    across = (
        (block_len + col_ids - row_ids < jnp.minimum(width_here, width_after))
        & jnp.logical_not(before_cut)
        & (col_ids < cut_after)
    )
    return (inside, across)


def curvature_sum(direction, image_vec):
    return lax.psum(jnp.sum(direction * image_vec, axis=1), ("genome", "ancestry"))


def residual_norm(residual, precond):
    return lax.psum(jnp.sum(residual * precond, axis=1), ("genome", "ancestry"))


def body(zscores, ld_diag, ld_next, prior_precision, chrom_cut, band_width):
    block_len = ld_diag.shape[1]
    block_count = lax.axis_size("genome")
    position = lax.axis_index("genome")
    ancestry_id = lax.axis_index("ancestry")
    following = jnp.minimum(position + 1, block_count - 1)
    inside, across = block_masks(
        block_len,
        chrom_cut[position],
        chrom_cut[following],
        band_width[position],
        band_width[following],
    )
    zero_value = jnp.zeros((), jnp.bfloat16)
    diag_tile = jnp.where(inside, ld_diag[0], zero_value)
    next_tile = jnp.where(across, ld_next[0], zero_value)
    prior_row = lax.dynamic_index_in_dim(prior_precision, ancestry_id, 0, keepdims=False)
    self_weight = lax.dynamic_index_in_dim(prior_row, ancestry_id, 0, keepdims=False)
    scaling = 1.0 / (jnp.diagonal(ld_diag[0]).astype(jnp.float32) + self_weight)
    residual = zscores[0]
    solution = jnp.zeros(residual.shape, jnp.float32)
    precond = scaling[None, :] * residual
    direction = precond
    norm_now = residual_norm(residual, precond)
    for iteration in range(ITERS):
        direction_bf = direction.astype(jnp.bfloat16)
        band_out = jnp.dot(direction_bf, diag_tile, preferred_element_type=jnp.float32)
        upper_part = passed_along(direction_bf, "genome", -1)
        band_out = band_out + lax.dot_general(
            upper_part, next_tile, (((1,), (1,)), ((), ())), preferred_element_type=jnp.float32
        )
        carried = jnp.dot(direction_bf, next_tile, preferred_element_type=jnp.float32)
        band_out = band_out + passed_along(carried.astype(jnp.bfloat16), "genome", 1).astype(
            carried.dtype
        )
        coupled = jnp.einsum(
            "b,btv->tv",
            prior_row,
            lax.all_gather(direction_bf[None], "ancestry", axis=0, tiled=True).astype(jnp.float32),
            precision=lax.Precision.HIGHEST,
        )
        image_vec = band_out + coupled
        step_len = norm_now / curvature_sum(direction, image_vec)
        solution = solution + step_len[:, None] * direction
        if iteration + 1 < ITERS:
            residual = residual - step_len[:, None] * image_vec
            precond = scaling[None, :] * residual
            norm_next = residual_norm(residual, precond)
            direction = precond + (norm_next / norm_now)[:, None] * direction
            norm_now = norm_next
    return solution[None]


def solution(mesh):
    return jax.shard_map(
        body,
        mesh=mesh,
        in_specs=(
            P("ancestry", "trait", ("groups", "genome")),
            P("ancestry", ("groups", "genome"), None),
            P("ancestry", ("groups", "genome"), None),
            P(),
            P("groups"),
            P("groups"),
        ),
        out_specs=P("ancestry", "trait", ("groups", "genome")),
        check_vma=False,
    )
```

profile of v0, /device:TPU:0, one launch (start us, length us, event | category | flops | bytes accessed | tf_op | source)
XLA Modules:
  0.0 168.3 jit_solution(2433427531543962618)
XLA Ops:
  0.0 1.4 dynamic_slice.20
  1.4 16.1 %gather_fusion = bf16[1024]{0:T(1024)(128)(2,1)S(1)} fusion(bf16[1024,1024]{1,0:T(8,128)(2,1)} %bitcast.66, s32[1024]{0:T(1024)S(1)} %bitcast.65), kind=kCustom, calls=%fused_computation | custom fusion | bytes 12288 | tf_op jit(solution)/shard_map/jit(diagonal)/cond/branch_0_fun/gather | solution.py:56
  17.6 0.7 add_divide_fusion
  18.3 1.3 collective-permute-start
  19.6 0.7 fusion.55
  20.3 0.6 iota_compare_fusion
  21.6 0.7 fusion.50
  23.5 0.0 copy-start.4
  23.5 1.2 fusion.27
  24.7 5.6 %collective-permute-start.1 = (bf16[32,1024]{1,0:T(8,128)(2,1)S(1)}, bf16[32,1024]{1,0:T(8,128)(2,1)S(1)}, u32[]{:S(2)}, u32[]{:S(2)}) collective-permute-start(bf16[32,1024]{1,0:T(8,128)(2,1)S(1)} %fusion.27), channel_id=1, source_target_pairs={{0,4},{4,8},{8,12},{1,5},{5,9},{9,13},{2,6},{6,10},{10,14},{3,7},{... | collective-permute-start | bytes 196616 | tf_op jit(solution)/shard_map/ppermute | solution.py:12
  30.3 0.7 fusion.48
  31.0 4.9 %all_gather.9 = bf16[2,32,1024]{2,1,0:T(8,128)(2,1)S(1)} all-gather(bf16[1,32,1024]{2,1,0:T(8,128)(2,1)S(1)} %multiply_convert_fusion.1), channel_id=1, replica_groups=mesh['groups'=2,'genome'=4,'ancestry'=2,'trait'=2] {'ancestry'}, dimensions={0}, use_global_device_ids=true | all-gather | bytes 196608 | tf_op jit(solution)/shard_map/all_gather | solution.py:76
  35.9 1.2 fusion.6
  37.1 0.4 copy-done.1
  37.5 1.9 %fusion.14 = f32[32,1024]{1,0:T(8,128)S(1)} fusion(bf16[1,1024,1024]{2,1,0:T(8,128)(2,1)S(1)} %copy-done.1, s32[]{:T(128)} %bitcast.5, pred[1024]{0:T(1024)(128)(4,1)S(1)} %fusion.48, bf16[1,32,1024]{2,1,0:T(8,128)(2,1)S(1)} %multiply_convert_fusion.1), kind=kOutput, calls=%fused_computation.18 | convolution fusion | flops 73400320 | bytes 2294788 | tf_op jit(solution)/shard_map/dot_general | solution.py:64
  39.4 0.0 copy-start.7
  39.4 3.1 %fusion.2 = bf16[1024,1024]{1,0:T(8,128)(2,1)} fusion(s32[]{:T(128)} %bitcast.5, pred[1024]{0:T(1024)(128)(4,1)S(1)} %fusion.48, bf16[1,1024,1024]{2,1,0:T(8,128)(2,1)S(1)} %copy-done.1), kind=kLoop, calls=%fused_computation.7 | loop fusion | flops 6291456 | bytes 4195332 | tf_op jit(solution)/shard_map/jit(_where)/select_n | solution.py:52
  42.5 0.6 fusion.44
  43.1 0.0 collective-permute-done
  43.1 0.0 collective-permute-done.1
  43.1 0.9 fusion.34
  44.0 19.9 %all-reduce = (f32[32]{0:T(128)S(1)}, f32[32]{0:T(128)S(1)}) all-reduce(f32[32]{0:T(128)S(1)} %get-tuple-element.6, f32[32]{0:T(128)S(1)} %get-tuple-element.5), channel_id=1, replica_groups=mesh['groups'=2,'genome'=4,'ancestry'=2,'trait'=2] {'genome','ancestry'}, use_global_device_ids=true, to_apply=%region_1.2 | all-reduce | flops 64 | bytes 512 | tf_op jit(solution)/shard_map/psum | solution.py:35
  63.9 0.2 fusion.38
  64.1 17.1 %psum.44 = f32[32]{0:T(128)S(1)} all-reduce(f32[32]{0:T(128)S(1)} %get-tuple-element.13), channel_id=1, replica_groups=mesh['groups'=2,'genome'=4,'ancestry'=2,'trait'=2] {'genome','ancestry'}, use_global_device_ids=true, to_apply=%region_5.6 | all-reduce | flops 32 | bytes 256 | tf_op jit(solution)/shard_map/psum | solution.py:35
  81.2 0.1 fusion.54
  81.3 0.5 convolution_convert_fusion.1
  81.8 1.4 collective-permute-start.2
  83.2 5.0 %all-gather = bf16[64,1024]{1,0:T(8,128)(2,1)S(1)} all-gather(bf16[32,1024]{1,0:T(8,128)(2,1)S(1)} %get-tuple-element.11), channel_id=2, replica_groups=mesh['groups'=2,'genome'=4,'ancestry'=2,'trait'=2] {'ancestry'}, dimensions={0}, use_global_device_ids=true | all-gather | bytes 196608 | tf_op jit(solution)/shard_map/all_gather | solution.py:76
  88.2 4.5 %collective-permute-start.3 = (bf16[32,1024]{1,0:T(8,128)(2,1)S(1)}, bf16[32,1024]{1,0:T(8,128)(2,1)S(1)}, u32[]{:S(2)}, u32[]{:S(2)}) collective-permute-start(bf16[32,1024]{1,0:T(8,128)(2,1)S(1)} %convolution_convert_fusion.1), channel_id=1, source_target_pairs={{0,4},{4,8},{8,12},{1,5},{5,9},{9,13},{2,6},{6,10},{10,14},{3,7},{... | collective-permute-start | bytes 196616 | tf_op jit(solution)/shard_map/ppermute | solution.py:12
  92.8 0.5 fusion.57
  93.2 0.6 fusion.42
  93.8 0.8 collective-permute-done.3
  94.7 0.0 collective-permute-done.2
  94.7 0.8 multiply_reduce_fusion
  95.5 19.2 %psum.45 = f32[32]{0:T(128)S(1)} all-reduce(f32[32]{0:T(128)S(1)} %get-tuple-element.20), channel_id=1, replica_groups=mesh['groups'=2,'genome'=4,'ancestry'=2,'trait'=2] {'genome','ancestry'}, use_global_device_ids=true, to_apply=%region_7.8 | all-reduce | flops 32 | bytes 256 | tf_op jit(solution)/shard_map/psum | solution.py:31
  114.8 0.2 fusion.39
  115.0 17.2 %psum.46 = f32[32]{0:T(128)S(1)} all-reduce(f32[32]{0:T(128)S(1)} %fusion.39), channel_id=1, replica_groups=mesh['groups'=2,'genome'=4,'ancestry'=2,'trait'=2] {'genome','ancestry'}, use_global_device_ids=true, to_apply=%region_9.10 | all-reduce | flops 32 | bytes 256 | tf_op jit(solution)/shard_map/psum | solution.py:35
  132.2 0.1 fusion.53
  132.3 2.1 %fusion.58 = f32[32,1024]{1,0:T(8,128)S(1)} fusion(bf16[32,1024]{1,0:T(8,128)(2,1)S(1)} %get-tuple-element.9, bf16[1024,1024]{1,0:T(8,128)(2,1)} %fusion.2), kind=kOutput, calls=%fused_computation.84 | convolution fusion | flops 67108864 | bytes 2293760 | tf_op jit(solution)/shard_map/dot_general | solution.py:64
  134.4 0.5 convolution_convert_fusion
  134.8 1.3 collective-permute-start.4
  136.1 5.0 %all-gather.1 = bf16[64,1024]{1,0:T(8,128)(2,1)S(1)} all-gather(bf16[32,1024]{1,0:T(8,128)(2,1)S(1)} %get-tuple-element.9), channel_id=3, replica_groups=mesh['groups'=2,'genome'=4,'ancestry'=2,'trait'=2] {'ancestry'}, dimensions={0}, use_global_device_ids=true | all-gather | bytes 196608 | tf_op jit(solution)/shard_map/all_gather | solution.py:76
  141.1 4.5 %collective-permute-start.5 = (bf16[32,1024]{1,0:T(8,128)(2,1)S(1)}, bf16[32,1024]{1,0:T(8,128)(2,1)S(1)}, u32[]{:S(2)}, u32[]{:S(2)}) collective-permute-start(bf16[32,1024]{1,0:T(8,128)(2,1)S(1)} %convolution_convert_fusion), channel_id=1, source_target_pairs={{0,4},{4,8},{8,12},{1,5},{5,9},{9,13},{2,6},{6,10},{10,14},{3,7},{... | collective-permute-start | bytes 196616 | tf_op jit(solution)/shard_map/ppermute | solution.py:12
  145.6 0.6 fusion.40
  146.2 1.3 collective-permute-done.5
  147.5 0.8 fusion.30
  148.4 19.1 %psum.47 = f32[32]{0:T(128)S(1)} all-reduce(f32[32]{0:T(128)S(1)} %fusion.30), channel_id=1, replica_groups=mesh['groups'=2,'genome'=4,'ancestry'=2,'trait'=2] {'genome','ancestry'}, use_global_device_ids=true, to_apply=%region_11.12 | all-reduce | flops 32 | bytes 256 | tf_op jit(solution)/shard_map/psum | solution.py:31
  167.5 0.8 fusion.37
  (23 shorter events, 0.1 us)
Async XLA Ops:
  0.0 18.2 %copy-start.2 = (f32[1,32,1024]{2,1,0:T(8,128)S(1)}, f32[1,32,1024]{2,1,0:T(8,128)}, u32[]{:S(2)}) copy-start(f32[1,32,1024]{2,1,0:T(8,128)} %param.6) | copy-start | bytes 393220
  0.0 19.6 %copy-start.6 = (s32[4]{0:T(128)S(1)}, s32[4]{0:T(128)}, u32[]{:S(2)}) copy-start(s32[4]{0:T(128)} %param.11) | copy-start | bytes 52
  0.0 19.6 %copy-start.5 = (s32[4]{0:T(128)S(1)}, s32[4]{0:T(128)}, u32[]{:S(2)}) copy-start(s32[4]{0:T(128)} %param.10) | copy-start | bytes 52
  0.0 23.5 %copy-start.3 = (bf16[1,1024,1024]{2,1,0:T(8,128)(2,1)S(1)}, bf16[1,1024,1024]{2,1,0:T(8,128)(2,1)}, u32[]{:S(2)}) copy-start(bf16[1,1024,1024]{2,1,0:T(8,128)(2,1)} %param.8) | copy-start | bytes 6291460
  18.3 24.8 %collective-permute-start = (bf16[32,1024]{1,0:T(8,128)(2,1)S(1)}, bf16[32,1024]{1,0:T(8,128)(2,1)S(1)}, u32[]{:S(2)}, u32[]{:S(2)}) collective-permute-start(bf16[32,1024]{1,0:T(8,128)(2,1)S(1)} %multiply_convert_fusion), channel_id=1, source_target_pairs={{4,0},{8,4},{12,8},{5,1},{9,5},{13,9},{6,2},{10,6},{14,10},{7,3},{... | collective-permute-start | bytes 196616 | tf_op jit(solution)/shard_map/ppermute | solution.py:12
  23.5 12.4 %copy-start.4 = (bf16[1,1024,1024]{2,1,0:T(8,128)(2,1)S(1)}, bf16[1,1024,1024]{2,1,0:T(8,128)(2,1)}, u32[]{:S(2)}) copy-start(bf16[1,1024,1024]{2,1,0:T(8,128)(2,1)} %param.8) | copy-start | bytes 6291460
  24.7 18.4 %collective-permute-start.1 = (bf16[32,1024]{1,0:T(8,128)(2,1)S(1)}, bf16[32,1024]{1,0:T(8,128)(2,1)S(1)}, u32[]{:S(2)}, u32[]{:S(2)}) collective-permute-start(bf16[32,1024]{1,0:T(8,128)(2,1)S(1)} %fusion.27), channel_id=1, source_target_pairs={{0,4},{4,8},{8,12},{1,5},{5,9},{9,13},{2,6},{6,10},{10,14},{3,7},{... | collective-permute-start | bytes 196616 | tf_op jit(solution)/shard_map/ppermute | solution.py:12
  35.9 1.6 copy-start.1
  39.4 3.1 %copy-start.7 = (f32[2,2]{1,0:T(2,128)S(1)}, f32[2,2]{1,0:T(2,128)}, u32[]{:S(2)}) copy-start(f32[2,2]{1,0:T(2,128)} %param.9) | copy-start | bytes 52
  81.2 11.6 %copy-start = (bf16[1024,1024]{1,0:T(8,128)(2,1)S(1)}, bf16[1024,1024]{1,0:T(8,128)(2,1)}, u32[]{:S(2)}) copy-start(bf16[1024,1024]{1,0:T(8,128)(2,1)} %fusion.2) | copy-start | bytes 6291460
  81.8 12.9 %collective-permute-start.2 = (bf16[32,1024]{1,0:T(8,128)(2,1)S(1)}, bf16[32,1024]{1,0:T(8,128)(2,1)S(1)}, u32[]{:S(2)}, u32[]{:S(2)}) collective-permute-start(bf16[32,1024]{1,0:T(8,128)(2,1)S(1)} %get-tuple-element.11), channel_id=1, source_target_pairs={{4,0},{8,4},{12,8},{5,1},{9,5},{13,9},{6,2},{10,6},{14,10},{7,3},{... | collective-permute-start | bytes 196616 | tf_op jit(solution)/shard_map/ppermute | solution.py:12
  88.2 6.4 %collective-permute-start.3 = (bf16[32,1024]{1,0:T(8,128)(2,1)S(1)}, bf16[32,1024]{1,0:T(8,128)(2,1)S(1)}, u32[]{:S(2)}, u32[]{:S(2)}) collective-permute-start(bf16[32,1024]{1,0:T(8,128)(2,1)S(1)} %convolution_convert_fusion.1), channel_id=1, source_target_pairs={{0,4},{4,8},{8,12},{1,5},{5,9},{9,13},{2,6},{6,10},{10,14},{3,7},{... | collective-permute-start | bytes 196616 | tf_op jit(solution)/shard_map/ppermute | solution.py:12
  134.8 12.7 %collective-permute-start.4 = (bf16[32,1024]{1,0:T(8,128)(2,1)S(1)}, bf16[32,1024]{1,0:T(8,128)(2,1)S(1)}, u32[]{:S(2)}, u32[]{:S(2)}) collective-permute-start(bf16[32,1024]{1,0:T(8,128)(2,1)S(1)} %get-tuple-element.9), channel_id=1, source_target_pairs={{4,0},{8,4},{12,8},{5,1},{9,5},{13,9},{6,2},{10,6},{14,10},{7,3},{... | collective-permute-start | bytes 196616 | tf_op jit(solution)/shard_map/ppermute | solution.py:12
  141.1 6.4 %collective-permute-start.5 = (bf16[32,1024]{1,0:T(8,128)(2,1)S(1)}, bf16[32,1024]{1,0:T(8,128)(2,1)S(1)}, u32[]{:S(2)}, u32[]{:S(2)}) collective-permute-start(bf16[32,1024]{1,0:T(8,128)(2,1)S(1)} %convolution_convert_fusion), channel_id=1, source_target_pairs={{0,4},{4,8},{8,12},{1,5},{5,9},{9,13},{2,6},{6,10},{10,14},{3,7},{... | collective-permute-start | bytes 196616 | tf_op jit(solution)/shard_map/ppermute | solution.py:12
where the time goes:
time: 169 us; the launch traced here: 168 us
  blocking collectives  108 us (64%)
  local copies, waits for them, and re-layouts  18.6 us (11%)
  starting transfers between devices  18.6 us (11%)
  matrix products  10.7 us (6%)
  other arithmetic  8.43 us (5%)
  waiting for transfers between devices  2.16 us (1%)
  between operations  2.13 us (1%)
    psum x3, blocking collectives, residual_norm(): return lax.psum(jnp.sum(residual * precond, axis=1), ('genome', 'ancestry'))  54.3 us
    psum x2, blocking collectives, curvature_sum(): lax.psum(jnp.sum(direction * image_vec, axis=1), ('genome', 'ancestry'))  38.4 us
    ppermute x6, starting transfers between devices, passed_along(): lax.ppermute(value, axis, [(source, source + steps) for source in range(l...  18.6 us
    gather x1, local copies, waits for them, and re-layouts, body(): scaling = 1.0 / (jnp.diagonal(ld_diag[0]).astype(jnp.float32) + self_weight)  16.1 us
    all_gather x3, blocking collectives, body(): lax.all_gather(direction_bf[None], 'ancestry', axis=0, tiled=True)  14.9 us
    dot_general x3, matrix products, body(): jnp.dot(direction_bf, diag_tile, preferred_element_type=jnp.float32)  4.38 us
  transfers between devices with their start and end apart: 6, of which 2 were waited for; matrix products, arithmetic and copies ran while one was open for 7% of the time, Pallas kernels for 0%

commit v1 on v0

--- a/solution.py
+++ b/solution.py
@@ -1,9 +1,19 @@
+import functools
 import jax
 import jax.numpy as jnp
 from jax import lax
 from jax.sharding import PartitionSpec as P
 
 ITERS = 3
+
+
+def _prepare_record(tile_in, axis_name, net_axis):
+    for dev in (axis_name, net_axis):
+        tile_in = jax.lax.psum(tile_in, dev)
+    return tile_in
+
+
+change_the_edge = functools.partial(_prepare_record, axis_name="ancestry", net_axis="genome")
 
 
 def passed_along(value, axis, steps):
@@ -28,7 +38,7 @@
 
 
 def curvature_sum(direction, image_vec):
-    return lax.psum(jnp.sum(direction * image_vec, axis=1), ("genome", "ancestry"))
+    return change_the_edge(jnp.sum(direction * image_vec, axis=1))
 
 
 def residual_norm(residual, precond):

time: 169 us -> 178 us (1.053)
  blocking collectives: 108 us -> 116 us
    psum x2 -> x6, blocking collectives: 38.4 us -> 46.6 us  [_prepare_record(): tile_in = jax.lax.psum(tile_in, dev)]
where the time goes in v1:
time: 178 us; the launch traced here: 177 us
  blocking collectives  116 us (65%)
  starting transfers between devices  18.7 us (11%)
  local copies, waits for them, and re-layouts  18.6 us (10%)
  matrix products  10.7 us (6%)
  other arithmetic  8.43 us (5%)
  waiting for transfers between devices  2.16 us (1%)
  between operations  2.13 us (1%)
    psum x3, blocking collectives, residual_norm(): return lax.psum(jnp.sum(residual * precond, axis=1), ('genome', 'ancestry'))  55 us
    psum x6, blocking collectives, _prepare_record(): tile_in = jax.lax.psum(tile_in, dev)  46.6 us
    ppermute x6, starting transfers between devices, passed_along(): lax.ppermute(value, axis, [(source, source + steps) for source in range(l...  18.7 us
    gather x1, local copies, waits for them, and re-layouts, body(): scaling = 1.0 / (jnp.diagonal(ld_diag[0]).astype(jnp.float32) + self_weight)  16.1 us
    all_gather x3, blocking collectives, body(): lax.all_gather(direction_bf[None], 'ancestry', axis=0, tiled=True)  14.8 us
    dot_general x3, matrix products, body(): jnp.dot(direction_bf, diag_tile, preferred_element_type=jnp.float32)  4.38 us
  transfers between devices with their start and end apart: 6, of which 2 were waited for; matrix products, arithmetic and copies ran while one was open for 7% of the time, Pallas kernels for 0%

profile of v1, /device:TPU:0, one launch (start us, length us, event | category | flops | bytes accessed | tf_op | source)
XLA Modules:
  0.0 177.1 jit_solution(5253529585163465881)
XLA Ops:
  0.0 1.4 dynamic_slice.20
  1.4 16.1 %gather_fusion = bf16[1024]{0:T(1024)(128)(2,1)S(1)} fusion(bf16[1024,1024]{1,0:T(8,128)(2,1)} %bitcast.66, s32[1024]{0:T(1024)S(1)} %bitcast.65), kind=kCustom, calls=%fused_computation | custom fusion | bytes 12288 | tf_op jit(solution)/shard_map/jit(diagonal)/cond/branch_0_fun/gather | solution.py:66
  17.6 0.7 add_divide_fusion
  18.3 1.3 collective-permute-start
  19.6 0.7 fusion.55
  20.3 0.6 iota_compare_fusion
  21.6 0.7 fusion.50
  23.5 0.0 copy-start.4
  23.5 1.2 fusion.27
  24.7 5.6 %collective-permute-start.1 = (bf16[32,1024]{1,0:T(8,128)(2,1)S(1)}, bf16[32,1024]{1,0:T(8,128)(2,1)S(1)}, u32[]{:S(2)}, u32[]{:S(2)}) collective-permute-start(bf16[32,1024]{1,0:T(8,128)(2,1)S(1)} %fusion.27), channel_id=1, source_target_pairs={{0,4},{4,8},{8,12},{1,5},{5,9},{9,13},{2,6},{6,10},{10,14},{3,7},{... | collective-permute-start | bytes 196616 | tf_op jit(solution)/shard_map/ppermute | solution.py:22
  30.3 0.7 fusion.48
  31.0 4.9 %all_gather.9 = bf16[2,32,1024]{2,1,0:T(8,128)(2,1)S(1)} all-gather(bf16[1,32,1024]{2,1,0:T(8,128)(2,1)S(1)} %multiply_convert_fusion.1), channel_id=1, replica_groups=mesh['groups'=2,'genome'=4,'ancestry'=2,'trait'=2] {'ancestry'}, dimensions={0}, use_global_device_ids=true | all-gather | bytes 196608 | tf_op jit(solution)/shard_map/all_gather | solution.py:86
  35.9 1.2 fusion.6
  37.1 0.4 copy-done.1
  37.5 1.9 %fusion.14 = f32[32,1024]{1,0:T(8,128)S(1)} fusion(bf16[1,1024,1024]{2,1,0:T(8,128)(2,1)S(1)} %copy-done.1, s32[]{:T(128)} %bitcast.5, pred[1024]{0:T(1024)(128)(4,1)S(1)} %fusion.48, bf16[1,32,1024]{2,1,0:T(8,128)(2,1)S(1)} %multiply_convert_fusion.1), kind=kOutput, calls=%fused_computation.18 | convolution fusion | flops 73400320 | bytes 2294788 | tf_op jit(solution)/shard_map/dot_general | solution.py:74
  39.4 3.1 %fusion.2 = bf16[1024,1024]{1,0:T(8,128)(2,1)} fusion(s32[]{:T(128)} %bitcast.5, pred[1024]{0:T(1024)(128)(4,1)S(1)} %fusion.48, bf16[1,1024,1024]{2,1,0:T(8,128)(2,1)S(1)} %copy-done.1), kind=kLoop, calls=%fused_computation.7 | loop fusion | flops 6291456 | bytes 4195332 | tf_op jit(solution)/shard_map/jit(_where)/select_n | solution.py:62
  42.5 0.6 fusion.44
  43.1 0.9 fusion.34
  44.0 4.9 %psum.64 = f32[32]{0:T(128)S(1)} all-reduce(f32[32]{0:T(128)S(1)} %get-tuple-element.5), channel_id=1, replica_groups=mesh['groups'=2,'genome'=4,'ancestry'=2,'trait'=2] {'ancestry'}, use_global_device_ids=true, to_apply=%region_3.4 | all-reduce | flops 32 | bytes 256 | tf_op jit(solution)/shard_map/psum | solution.py:12
  48.9 10.3 %psum.65 = f32[32]{0:T(128)S(1)} all-reduce(f32[32]{0:T(128)S(1)} %psum.64), channel_id=1, replica_groups=mesh['groups'=2,'genome'=4,'ancestry'=2,'trait'=2] {'genome'}, use_global_device_ids=true, to_apply=%region_4.5 | all-reduce | flops 32 | bytes 256 | tf_op jit(solution)/shard_map/psum | solution.py:12
  59.3 18.7 %psum.63 = f32[32]{0:T(128)S(1)} all-reduce(f32[32]{0:T(128)S(1)} %get-tuple-element.6), channel_id=1, replica_groups=mesh['groups'=2,'genome'=4,'ancestry'=2,'trait'=2] {'genome','ancestry'}, use_global_device_ids=true, to_apply=%region_1.2 | all-reduce | flops 32 | bytes 256 | tf_op jit(solution)/shard_map/psum | solution.py:45
  78.0 0.2 fusion.38
  78.2 17.5 %psum.66 = f32[32]{0:T(128)S(1)} all-reduce(f32[32]{0:T(128)S(1)} %get-tuple-element.11), channel_id=1, replica_groups=mesh['groups'=2,'genome'=4,'ancestry'=2,'trait'=2] {'genome','ancestry'}, use_global_device_ids=true, to_apply=%region_6.7 | all-reduce | flops 32 | bytes 256 | tf_op jit(solution)/shard_map/psum | solution.py:45
  95.7 0.1 fusion.54
  95.8 0.5 convolution_convert_fusion.1
  96.3 1.4 collective-permute-start.2
  97.7 4.9 %all-gather = bf16[64,1024]{1,0:T(8,128)(2,1)S(1)} all-gather(bf16[32,1024]{1,0:T(8,128)(2,1)S(1)} %get-tuple-element.9), channel_id=2, replica_groups=mesh['groups'=2,'genome'=4,'ancestry'=2,'trait'=2] {'ancestry'}, dimensions={0}, use_global_device_ids=true | all-gather | bytes 196608 | tf_op jit(solution)/shard_map/all_gather | solution.py:86
  102.7 4.5 %collective-permute-start.3 = (bf16[32,1024]{1,0:T(8,128)(2,1)S(1)}, bf16[32,1024]{1,0:T(8,128)(2,1)S(1)}, u32[]{:S(2)}, u32[]{:S(2)}) collective-permute-start(bf16[32,1024]{1,0:T(8,128)(2,1)S(1)} %convolution_convert_fusion.1), channel_id=1, source_target_pairs={{0,4},{4,8},{8,12},{1,5},{5,9},{9,13},{2,6},{6,10},{10,14},{3,7},{... | collective-permute-start | bytes 196616 | tf_op jit(solution)/shard_map/ppermute | solution.py:22
  107.2 0.5 fusion.57
  107.7 0.6 fusion.42
  108.3 0.8 collective-permute-done.3
  109.1 0.8 multiply_reduce_fusion
  109.9 4.9 %psum.67 = f32[32]{0:T(128)S(1)} all-reduce(f32[32]{0:T(128)S(1)} %get-tuple-element.18), channel_id=1, replica_groups=mesh['groups'=2,'genome'=4,'ancestry'=2,'trait'=2] {'ancestry'}, use_global_device_ids=true, to_apply=%region_8.9 | all-reduce | flops 32 | bytes 256 | tf_op jit(solution)/shard_map/psum | solution.py:12
  114.9 10.7 %psum.68 = f32[32]{0:T(128)S(1)} all-reduce(f32[32]{0:T(128)S(1)} %psum.67), channel_id=1, replica_groups=mesh['groups'=2,'genome'=4,'ancestry'=2,'trait'=2] {'genome'}, use_global_device_ids=true, to_apply=%region_9.10 | all-reduce | flops 32 | bytes 256 | tf_op jit(solution)/shard_map/psum | solution.py:12
  125.6 0.2 fusion.39
  125.8 18.7 %psum.69 = f32[32]{0:T(128)S(1)} all-reduce(f32[32]{0:T(128)S(1)} %fusion.39), channel_id=1, replica_groups=mesh['groups'=2,'genome'=4,'ancestry'=2,'trait'=2] {'genome','ancestry'}, use_global_device_ids=true, to_apply=%region_11.12 | all-reduce | flops 32 | bytes 256 | tf_op jit(solution)/shard_map/psum | solution.py:45
  144.5 0.1 fusion.53
  144.6 2.1 %fusion.58 = f32[32,1024]{1,0:T(8,128)S(1)} fusion(bf16[32,1024]{1,0:T(8,128)(2,1)S(1)} %get-tuple-element.7, bf16[1024,1024]{1,0:T(8,128)(2,1)} %fusion.2), kind=kOutput, calls=%fused_computation.84 | convolution fusion | flops 67108864 | bytes 2293760 | tf_op jit(solution)/shard_map/dot_general | solution.py:74
  146.7 0.5 convolution_convert_fusion
  147.2 1.3 collective-permute-start.4
  148.5 4.9 %all-gather.1 = bf16[64,1024]{1,0:T(8,128)(2,1)S(1)} all-gather(bf16[32,1024]{1,0:T(8,128)(2,1)S(1)} %get-tuple-element.7), channel_id=3, replica_groups=mesh['groups'=2,'genome'=4,'ancestry'=2,'trait'=2] {'ancestry'}, dimensions={0}, use_global_device_ids=true | all-gather | bytes 196608 | tf_op jit(solution)/shard_map/all_gather | solution.py:86
  153.4 4.5 %collective-permute-start.5 = (bf16[32,1024]{1,0:T(8,128)(2,1)S(1)}, bf16[32,1024]{1,0:T(8,128)(2,1)S(1)}, u32[]{:S(2)}, u32[]{:S(2)}) collective-permute-start(bf16[32,1024]{1,0:T(8,128)(2,1)S(1)} %convolution_convert_fusion), channel_id=1, source_target_pairs={{0,4},{4,8},{8,12},{1,5},{5,9},{9,13},{2,6},{6,10},{10,14},{3,7},{... | collective-permute-start | bytes 196616 | tf_op jit(solution)/shard_map/ppermute | solution.py:22
  158.0 0.6 fusion.40
  158.5 1.3 collective-permute-done.5
  159.9 0.8 fusion.30
  160.7 4.9 %psum.70 = f32[32]{0:T(128)S(1)} all-reduce(f32[32]{0:T(128)S(1)} %fusion.30), channel_id=1, replica_groups=mesh['groups'=2,'genome'=4,'ancestry'=2,'trait'=2] {'ancestry'}, use_global_device_ids=true, to_apply=%region_13.14 | all-reduce | flops 32 | bytes 256 | tf_op jit(solution)/shard_map/psum | solution.py:12
  165.6 10.7 %psum.71 = f32[32]{0:T(128)S(1)} all-reduce(f32[32]{0:T(128)S(1)} %psum.70), channel_id=1, replica_groups=mesh['groups'=2,'genome'=4,'ancestry'=2,'trait'=2] {'genome'}, use_global_device_ids=true, to_apply=%region_14.15 | all-reduce | flops 32 | bytes 256 | tf_op jit(solution)/shard_map/psum | solution.py:12
  176.3 0.8 fusion.37
  (27 shorter events, 0.1 us)
Async XLA Ops:
  0.0 18.2 %copy-start.2 = (f32[1,32,1024]{2,1,0:T(8,128)S(1)}, f32[1,32,1024]{2,1,0:T(8,128)}, u32[]{:S(2)}) copy-start(f32[1,32,1024]{2,1,0:T(8,128)} %param.6) | copy-start | bytes 393220
  0.0 19.6 %copy-start.6 = (s32[4]{0:T(128)S(1)}, s32[4]{0:T(128)}, u32[]{:S(2)}) copy-start(s32[4]{0:T(128)} %param.11) | copy-start | bytes 52
  0.0 19.6 %copy-start.5 = (s32[4]{0:T(128)S(1)}, s32[4]{0:T(128)}, u32[]{:S(2)}) copy-start(s32[4]{0:T(128)} %param.10) | copy-start | bytes 52
  0.0 23.5 %copy-start.3 = (bf16[1,1024,1024]{2,1,0:T(8,128)(2,1)S(1)}, bf16[1,1024,1024]{2,1,0:T(8,128)(2,1)}, u32[]{:S(2)}) copy-start(bf16[1,1024,1024]{2,1,0:T(8,128)(2,1)} %param.8) | copy-start | bytes 6291460
  18.3 24.8 %collective-permute-start = (bf16[32,1024]{1,0:T(8,128)(2,1)S(1)}, bf16[32,1024]{1,0:T(8,128)(2,1)S(1)}, u32[]{:S(2)}, u32[]{:S(2)}) collective-permute-start(bf16[32,1024]{1,0:T(8,128)(2,1)S(1)} %multiply_convert_fusion), channel_id=1, source_target_pairs={{4,0},{8,4},{12,8},{5,1},{9,5},{13,9},{6,2},{10,6},{14,10},{7,3},{... | collective-permute-start | bytes 196616 | tf_op jit(solution)/shard_map/ppermute | solution.py:22
  23.5 12.4 %copy-start.4 = (bf16[1,1024,1024]{2,1,0:T(8,128)(2,1)S(1)}, bf16[1,1024,1024]{2,1,0:T(8,128)(2,1)}, u32[]{:S(2)}) copy-start(bf16[1,1024,1024]{2,1,0:T(8,128)(2,1)} %param.8) | copy-start | bytes 6291460
  24.7 18.4 %collective-permute-start.1 = (bf16[32,1024]{1,0:T(8,128)(2,1)S(1)}, bf16[32,1024]{1,0:T(8,128)(2,1)S(1)}, u32[]{:S(2)}, u32[]{:S(2)}) collective-permute-start(bf16[32,1024]{1,0:T(8,128)(2,1)S(1)} %fusion.27), channel_id=1, source_target_pairs={{0,4},{4,8},{8,12},{1,5},{5,9},{9,13},{2,6},{6,10},{10,14},{3,7},{... | collective-permute-start | bytes 196616 | tf_op jit(solution)/shard_map/ppermute | solution.py:22
  35.9 1.6 copy-start.1
  39.4 3.1 %copy-start.7 = (f32[2,2]{1,0:T(2,128)S(1)}, f32[2,2]{1,0:T(2,128)}, u32[]{:S(2)}) copy-start(f32[2,2]{1,0:T(2,128)} %param.9) | copy-start | bytes 52
  95.7 11.5 %copy-start = (bf16[1024,1024]{1,0:T(8,128)(2,1)S(1)}, bf16[1024,1024]{1,0:T(8,128)(2,1)}, u32[]{:S(2)}) copy-start(bf16[1024,1024]{1,0:T(8,128)(2,1)} %fusion.2) | copy-start | bytes 6291460
  96.3 12.8 %collective-permute-start.2 = (bf16[32,1024]{1,0:T(8,128)(2,1)S(1)}, bf16[32,1024]{1,0:T(8,128)(2,1)S(1)}, u32[]{:S(2)}, u32[]{:S(2)}) collective-permute-start(bf16[32,1024]{1,0:T(8,128)(2,1)S(1)} %get-tuple-element.9), channel_id=1, source_target_pairs={{4,0},{8,4},{12,8},{5,1},{9,5},{13,9},{6,2},{10,6},{14,10},{7,3},{... | collective-permute-start | bytes 196616 | tf_op jit(solution)/shard_map/ppermute | solution.py:22
  102.7 6.4 %collective-permute-start.3 = (bf16[32,1024]{1,0:T(8,128)(2,1)S(1)}, bf16[32,1024]{1,0:T(8,128)(2,1)S(1)}, u32[]{:S(2)}, u32[]{:S(2)}) collective-permute-start(bf16[32,1024]{1,0:T(8,128)(2,1)S(1)} %convolution_convert_fusion.1), channel_id=1, source_target_pairs={{0,4},{4,8},{8,12},{1,5},{5,9},{9,13},{2,6},{6,10},{10,14},{3,7},{... | collective-permute-start | bytes 196616 | tf_op jit(solution)/shard_map/ppermute | solution.py:22
  147.2 12.7 %collective-permute-start.4 = (bf16[32,1024]{1,0:T(8,128)(2,1)S(1)}, bf16[32,1024]{1,0:T(8,128)(2,1)S(1)}, u32[]{:S(2)}, u32[]{:S(2)}) collective-permute-start(bf16[32,1024]{1,0:T(8,128)(2,1)S(1)} %get-tuple-element.7), channel_id=1, source_target_pairs={{4,0},{8,4},{12,8},{5,1},{9,5},{13,9},{6,2},{10,6},{14,10},{7,3},{... | collective-permute-start | bytes 196616 | tf_op jit(solution)/shard_map/ppermute | solution.py:22
  153.4 6.4 %collective-permute-start.5 = (bf16[32,1024]{1,0:T(8,128)(2,1)S(1)}, bf16[32,1024]{1,0:T(8,128)(2,1)S(1)}, u32[]{:S(2)}, u32[]{:S(2)}) collective-permute-start(bf16[32,1024]{1,0:T(8,128)(2,1)S(1)} %convolution_convert_fusion), channel_id=1, source_target_pairs={{0,4},{4,8},{8,12},{1,5},{5,9},{9,13},{2,6},{6,10},{10,14},{3,7},{... | collective-permute-start | bytes 196616 | tf_op jit(solution)/shard_map/ppermute | solution.py:22
